TPU v7x, 256 devices: a whole 4x4x8 slice. The times are simulated.
256 devices in a mesh: seq: 64 (over y, z, core), grp: 4 (over x).
Axes of the slice: x: 4, y: 4, z: 8, core: 2. Of those that a mesh axis runs over, the one named last changes fastest.
Arguments:
- doc_lengths: int32 [4, 16], P('grp'), may hold values from 1 to 1024, 8192 in all within a row
- hidden: bfloat16 [4, 8192, 7168], P('grp', 'seq'), may hold values from -16 to 16
- gate_weight: bfloat16 [7168, 64], P(('seq', 'grp')), may hold values from -0.0625 to 0.0625
- target_query: bfloat16 [4, 8192, 36864], P('grp', 'seq'), may hold values from -30 to 30
- latent_keys: bfloat16 [4, 8192, 576], P('grp', 'seq'), may hold values from -6 to 6
- index_query: bfloat16 [4, 8192, 8192], P('grp', 'seq'), may hold values from -15 to 15
- index_keys: bfloat16 [4, 8192, 128], P('grp', 'seq'), may hold values from -6 to 6
Outputs:
- divergence: float32 [4, 8192], P('grp', 'seq')
- grad_gate: float32 [7168, 64], P(('seq', 'grp'))
All inputs are finite; a program needn't handle non-finite values.
Results may differ from a plain program's by a relative error of at most 0.0022.
Values may be sent and summed in bfloat16 or wider, within the bound.
A program may use at most 128 MiB of HBM per device.

v0:
```python
import jax
import jax.numpy as jnp
from jax import lax
from jax.sharding import Mesh
from jax.sharding import PartitionSpec as P

LOOK = 8
SEQ = ("seq_0", "seq_1", "seq_2")
SEQ_GRP = ("seq_0", "seq_1", "seq_2", "grp")
target_scale = 0.07216878364870322
highest = lax.Precision.HIGHEST
floor_value = -1e30


def shifted(block, axis, distance):
    devices = range(lax.axis_size(axis))
    route = [(i - distance, i) for i in devices if i - distance in devices]
    return lax.ppermute(block, axis, route)


def reduced_to_own(blocks, axes, sequence):
    inside = blocks.shape[1:]
    blocks = blocks.reshape(*(lax.axis_size(a) for a in axes), *inside)
    blocks = jnp.moveaxis(blocks, sequence, range(len(axes))).reshape(-1, *inside)
    for k in sequence:
        blocks = lax.psum_scatter(blocks, axes[k], scatter_dimension=0, tiled=True)
    return blocks[0]


def split_up(value, dim, peers):
    lengths = value.shape
    blocks = value.reshape(*lengths[:dim], peers, lengths[dim] // peers, *lengths[dim + 1 :])
    return jnp.moveaxis(blocks, dim, 0)


def scatter_axes(value, axes, sequence, dim):
    peers = lax.axis_size(axes)
    return reduced_to_own(split_up(value, dim, peers), axes, sequence)


def piece_terms(
    target_rows,
    index_rows,
    gate_rows,
    latent_panel,
    index_panel,
    panel_start_offset,
    positions,
    lengths,
    doc_most,
):
    piece_count, piece_rows = positions.shape
    latent_width = latent_panel.shape[1]
    index_width = index_panel.shape[1]
    key_tile = 128
    span_keys = (doc_most + piece_rows - 1 + key_tile - 1) // key_tile * key_tile
    doc_ends = jnp.cumsum(lengths)
    starts = jnp.sum(lengths * (doc_ends <= positions[..., None]).astype(jnp.int32), -1)
    tile_counts = (positions[:, -1] + 1 - starts[:, 0] + key_tile - 1) // key_tile
    ranking = jnp.argsort(tile_counts, stable=True)
    batch_pieces = max(1, 16 // piece_rows)
    batch_count = piece_count // batch_pieces
    factor = index_width ** (-0.5)
    latent_padded = jnp.concatenate(
        [latent_panel, jnp.zeros((key_tile, latent_width), latent_panel.dtype)], 0
    )
    index_padded = jnp.concatenate(
        [index_panel, jnp.zeros((key_tile, index_width), index_panel.dtype)], 0
    )
    offsets = jnp.arange(key_tile, dtype=jnp.int32)

    def one_batch(batch_index):
        chosen = lax.dynamic_slice_in_dim(ranking, batch_index * batch_pieces, batch_pieces, 0)
        queries = jnp.take(target_rows, chosen, axis=0).reshape(
            batch_pieces, piece_rows, -1, latent_width
        )
        indexer_query_rows = jnp.take(index_rows, chosen, axis=0).reshape(
            batch_pieces, piece_rows, -1, index_width
        )
        gate_values = jnp.take(gate_rows, chosen, axis=0)
        row_pos = jnp.take(positions, chosen, axis=0)
        row_start = jnp.take(starts, chosen, axis=0)
        anchor = row_start[:, 0]
        turn_count = jnp.max(jnp.take(tile_counts, chosen, axis=0))
        head_count = queries.shape[2]
        gate_heads = gate_values.shape[2]

        def allowed_of(turn_index):
            key_pos = anchor[:, None] + turn_index * key_tile + offsets[None, :]
            return (key_pos[:, None, :] >= row_start[:, :, None]) & (
                key_pos[:, None, :] <= row_pos[:, :, None]
            )

        def cut_panel(first_key):
            return (
                lax.dynamic_slice_in_dim(
                    latent_padded, first_key - panel_start_offset, key_tile, 0
                ),
                lax.dynamic_slice_in_dim(index_padded, first_key - panel_start_offset, key_tile, 0),
            )

        def first_pass(turn_index, carry):
            logit_store, relu_store, head_peak, head_total, score_peak, score_total = carry
            latent_tile, indexer_key_block = jax.vmap(cut_panel)(anchor + turn_index * key_tile)
            allowed = allowed_of(turn_index)
            logits = (
                jnp.einsum(
                    "brhc,bkc->brhk", queries, latent_tile, preferred_element_type=jnp.float32
                )
                * target_scale
            )
            relu_score = jnp.maximum(
                jnp.einsum(
                    "fjme,fve->fjmv",
                    indexer_query_rows,
                    indexer_key_block,
                    preferred_element_type=jnp.float32,
                ),
                0.0,
            )
            score = factor * jnp.einsum("brh,brhk->brk", gate_values, relu_score, precision=highest)
            masked = jnp.where(allowed[:, :, None, :], logits, floor_value)
            new_peak = jnp.maximum(head_peak, jnp.max(masked, -1))
            head_total = head_total * jnp.exp(head_peak - new_peak) + jnp.sum(
                jnp.where(allowed[:, :, None, :], jnp.exp(masked - new_peak[..., None]), 0.0), -1
            )
            masked_score = jnp.where(allowed, score, floor_value)
            new_score_peak = jnp.maximum(score_peak, jnp.max(masked_score, -1))
            score_total = score_total * jnp.exp(score_peak - new_score_peak) + jnp.sum(
                jnp.where(allowed, jnp.exp(masked_score - new_score_peak[..., None]), 0.0), -1
            )
            logit_store = lax.dynamic_update_slice_in_dim(
                logit_store, logits, turn_index * key_tile, 3
            )
            relu_store = lax.dynamic_update_slice_in_dim(
                relu_store, relu_score, turn_index * key_tile, 3
            )
            return (logit_store, relu_store, new_peak, head_total, new_score_peak, score_total)

        start_carry = (
            jnp.zeros((batch_pieces, piece_rows, head_count, span_keys), jnp.float32),
            jnp.zeros((batch_pieces, piece_rows, gate_heads, span_keys), jnp.float32),
            jnp.full((batch_pieces, piece_rows, head_count), floor_value, jnp.float32),
            jnp.zeros((batch_pieces, piece_rows, head_count), jnp.float32),
            jnp.full((batch_pieces, piece_rows), floor_value, jnp.float32),
            jnp.zeros((batch_pieces, piece_rows), jnp.float32),
        )
        logit_store, relu_store, head_peak, head_total, score_peak, score_total = lax.fori_loop(
            0, turn_count, first_pass, start_carry
        )
        head_log = head_peak + jnp.log(head_total)
        score_log = score_peak + jnp.log(score_total)

        def second_pass(turn_index, carry):
            row_div, delta_terms = carry
            allowed = allowed_of(turn_index)
            logits = lax.dynamic_slice_in_dim(logit_store, turn_index * key_tile, key_tile, 3)
            relu_score = lax.dynamic_slice_in_dim(relu_store, turn_index * key_tile, key_tile, 3)
            probabilities = jnp.where(
                allowed[:, :, None, :], jnp.exp(logits - head_log[..., None]), 0.0
            )
            target = jnp.mean(probabilities, axis=2)
            score = factor * jnp.einsum("brh,brhk->brk", gate_values, relu_score, precision=highest)
            log_model = jnp.where(allowed, score - score_log[..., None], 0.0)
            model_prob = jnp.where(allowed, jnp.exp(log_model), 0.0)
            positive = target > 0
            target_log_probabilities = jnp.where(
                positive, target * jnp.log(jnp.where(positive, target, 1.0)), 0.0
            )
            row_div = row_div + jnp.sum(
                jnp.where(allowed, target_log_probabilities - target * log_model, 0.0), -1
            )
            delta_terms = delta_terms + factor * jnp.einsum(
                "brk,brhk->brh", model_prob - target, relu_score, precision=highest
            )
            return (row_div, delta_terms)

        return lax.fori_loop(
            0,
            turn_count,
            second_pass,
            (
                jnp.zeros((batch_pieces, piece_rows), jnp.float32),
                jnp.zeros((batch_pieces, piece_rows, gate_heads), jnp.float32),
            ),
        )

    sorted_div, sorted_delta = lax.map(one_batch, jnp.arange(batch_count, dtype=jnp.int32))
    sorted_div = sorted_div.reshape(piece_count, piece_rows)
    sorted_delta = sorted_delta.reshape(piece_count, piece_rows, -1)
    row_div = jnp.zeros_like(sorted_div).at[ranking].set(sorted_div)
    delta_terms = jnp.zeros_like(sorted_delta).at[ranking].set(sorted_delta)
    return (row_div, delta_terms)


def body(doc_lengths, hidden, gate_weight, target_query, latent_keys, index_query, index_keys):
    seq_count = lax.axis_size(SEQ)
    my_index = lax.axis_index(SEQ)
    row_count = hidden.shape[1]
    reach_devices = min(LOOK, seq_count // 2)
    doc_most = reach_devices * row_count
    lengths = doc_lengths[0]
    full_gate = lax.all_gather(gate_weight, SEQ_GRP, axis=0, tiled=True)
    block_rows = 16
    block_count = row_count // block_rows
    latent_parts = []
    index_parts = []
    for offset in range(reach_devices, 0, -1):
        latent_prev, index_prev = shifted((latent_keys[0], index_keys[0]), SEQ, offset)
        latent_parts.append(latent_prev)
        index_parts.append(index_prev)
    latent_win = jnp.concatenate(latent_parts + [latent_keys[0]], 0)
    index_win = jnp.concatenate(index_parts + [index_keys[0]], 0)
    panel_start_offset = my_index * row_count - doc_most
    positions = (my_index * row_count + jnp.arange(row_count, dtype=jnp.int32)).reshape(
        block_count, block_rows
    )
    gates_home = jnp.dot(hidden[0], full_gate, preferred_element_type=jnp.float32).reshape(
        block_count, block_rows, -1
    )
    row_div, delta_terms = piece_terms(
        target_query[0].reshape(block_count, block_rows, -1),
        index_query[0].reshape(block_count, block_rows, -1),
        gates_home,
        latent_win,
        index_win,
        panel_start_offset,
        positions,
        lengths,
        doc_most,
    )
    gate_delta = (delta_terms.reshape(row_count, -1) / row_count).astype(jnp.bfloat16)
    partial_value = jnp.dot(hidden[0].T, gate_delta, preferred_element_type=jnp.float32)
    divergence = row_div.reshape(1, row_count)
    grad_gate = scatter_axes(partial_value, SEQ_GRP, (2, 0, 1, 3), 0)
    return (divergence, grad_gate)


def solution(mesh):
    split = Mesh(
        mesh.devices.reshape(4, 8, 2, mesh.shape["grp"]), ("seq_0", "seq_1", "seq_2", "grp")
    )
    in_specs = (
        P("grp", None),
        P("grp", SEQ, None),
        P(SEQ_GRP, None),
        P("grp", SEQ, None),
        P("grp", SEQ, None),
        P("grp", SEQ, None),
        P("grp", SEQ, None),
    )
    out_specs = (P("grp", SEQ), P(SEQ_GRP, None))
    return jax.shard_map(body, mesh=split, in_specs=in_specs, out_specs=out_specs, check_vma=False)
```

profile of v0, /device:TPU:8, one launch (start us, length us, event | category | flops | bytes accessed | tf_op | source)
XLA Modules:
  0.0 1303.6 jit_solution(13120426017892355332)
XLA Ops:
  7.2 9.2 collective-permute-start
  22.5 7.1 collective-permute-start.3
  34.3 134.9 %all-gather = bf16[256,28,64]{2,1,0:T(8,128)(2,1)} all-gather(bf16[1,28,64]{2,1,0:T(8,128)(2,1)} %bitcast.295), channel_id=1, replica_groups=mesh['seq_0'=4,'seq_1'=8,'seq_2'=2,'grp'=4] {'seq_0','seq_1','seq_2','grp'}, dimensions={0}, use_global_device_ids=true | all-gather | bytes 921088 | tf_op jit(solution)/shard_map/all_gather | solution.py:203
  180.1 6.6 collective-permute-done.9
  188.7 7.8 collective-permute-done.10
  198.4 7.2 collective-permute-done.11
  207.5 6.9 collective-permute-done.12
  216.3 6.3 collective-permute-done.13
  257.5 263.1 %while.59 = (s32[]{:T(128)}, f32[8,1,16]{2,1,0:T(1,128)S(1)}, f32[8,1,16,64]{3,2,1,0:T(8,128)}, s32[8]{0:T(128)S(1)}, s32[8]{0:T(128)S(1)}, /*index=5*/s32[8]{0:...) while((s32[]{:T(128)}, f32[8,1,16]{2,1,0:T(1,128)S(1)}, ...), condition=%wide.region_14.16_spmd.clone.clone, body=%wide.region_3.15_spmd.clone.clone.sunk | while | flops 191511280 | bytes 22292232 | solution.py:188
  275.6 6.1 while.60
  305.6 6.1 while.60
  335.7 6.1 while.60
  365.8 6.1 while.60
  395.8 6.1 while.60
  425.9 6.1 while.60
  456.0 12.2 while.60
  468.2 10.4 while.61
  497.3 12.2 while.60
  509.6 10.4 while.61
  531.9 6.4 copy.26
  538.4 629.2 %reduce-scatter.5.cloned.1.call-done = f32[128,28,64]{2,0,1:T(8,128)} async-done(((f32[256,28,64]{2,0,1:T(8,128)}), f32[128,28,64]{2,0,1:T(8,128)}) %reduce-scatter.5.cloned.1.call-update) | async-done | bytes 917520 | tf_op jit(solution)/shard_map/reduce_scatter | solution.py:26
  1167.7 32.7 %reduce-scatter.7.cloned.1.call-done = f32[32,28,64]{2,0,1:T(8,128)} async-done(((f32[128,28,64]{2,0,1:T(8,128)}), f32[32,28,64]{2,0,1:T(8,128)}) %reduce-scatter.7.cloned.1.call-update) | async-done | bytes 229392 | tf_op jit(solution)/shard_map/reduce_scatter | solution.py:26
  1203.5 73.9 %all-reduce.4.cloned.1.call-done = f32[32,28,64]{2,0,1:T(8,128)} async-done(((f32[32,28,64]{2,0,1:T(8,128)}), f32[32,28,64]{2,0,1:T(8,128)}) %all-reduce.4.cloned.1.call-update) | async-done | bytes 229392
  1278.3 17.5 %all-reduce.1 = f32[4,28,64]{2,0,1:T(4,128)S(1)} all-reduce(f32[4,28,64]{2,0,1:T(4,128)S(1)} %constant_dynamic-slice_fusion.3), channel_id=5, replica_groups=mesh['seq_0'=4,'seq_1'=8,'seq_2'=2,'grp'=4] {'grp'}, use_global_device_ids=true, to_apply=%region_20.22.clone | all-reduce | flops 7168 | bytes 57344
  (513 shorter events, 333.5 us)
Async XLA Ops:
  7.2 167.0 %copy-start = (bf16[1,128,7168]{2,1,0:T(8,128)(2,1)S(1)}, bf16[1,128,7168]{2,1,0:T(8,128)(2,1)}, u32[]{:S(2)}) copy-start(bf16[1,128,7168]{2,1,0:T(8,128)(2,1)} %param.16) | copy-start | bytes 5505028
  7.2 1160.4 %reduce-scatter.5.cloned.1.call-start = ((), (), s32[]{:S(2)}) async-start(), calls=%async_computation.2 | async-start | bytes 5505024 | tf_op jit(solution)/shard_map/reduce_scatter | solution.py:26
  7.2 232.6 %collective-permute-start = (bf16[128,576]{0,1:T(8,128)(2,1)}, bf16[128,576]{0,1:T(8,128)(2,1)S(1)}, u32[]{:S(2)}, u32[]{:S(2)}) collective-permute-start(bf16[128,576]{0,1:T(8,128)(2,1)} %bitcast.276), channel_id=1, source_target_pairs={{0,32},{4,36},{8,40},{12,44},{16,48},{20,52},{24,56},{28,60},{32,6... | collective-permute-start | bytes 442376 | tf_op jit(solution)/shard_map/ppermute | solution.py:18
  16.5 226.1 %collective-permute-start.1 = (bf16[128,576]{0,1:T(8,128)(2,1)}, bf16[128,576]{0,1:T(8,128)(2,1)S(1)}, u32[]{:S(2)}, u32[]{:S(2)}) collective-permute-start(bf16[128,576]{0,1:T(8,128)(2,1)} %bitcast.277), channel_id=1, source_target_pairs={{0,28},{4,32},{8,36},{12,40},{16,44},{20,48},{24,52},{28,56},{32,6... | collective-permute-start | bytes 442376 | tf_op jit(solution)/shard_map/ppermute | solution.py:18
  19.5 225.0 %collective-permute-start.2 = (bf16[128,576]{0,1:T(8,128)(2,1)}, bf16[128,576]{0,1:T(8,128)(2,1)S(1)}, u32[]{:S(2)}, u32[]{:S(2)}) collective-permute-start(bf16[128,576]{0,1:T(8,128)(2,1)} %bitcast.278), channel_id=1, source_target_pairs={{0,24},{4,28},{8,32},{12,36},{16,40},{20,44},{24,48},{28,52},{32,5... | collective-permute-start | bytes 442376 | tf_op jit(solution)/shard_map/ppermute | solution.py:18
  22.5 224.2 %collective-permute-start.3 = (bf16[128,576]{0,1:T(8,128)(2,1)}, bf16[128,576]{0,1:T(8,128)(2,1)S(1)}, u32[]{:S(2)}, u32[]{:S(2)}) collective-permute-start(bf16[128,576]{0,1:T(8,128)(2,1)} %bitcast.279), channel_id=1, source_target_pairs={{0,20},{4,24},{8,28},{12,32},{16,36},{20,40},{24,44},{28,48},{32,5... | collective-permute-start | bytes 442376 | tf_op jit(solution)/shard_map/ppermute | solution.py:18
  29.6 146.8 %collective-permute-start.8 = (bf16[128,128]{1,0:T(8,128)(2,1)}, bf16[128,128]{1,0:T(8,128)(2,1)S(1)}, u32[]{:S(2)}, u32[]{:S(2)}) collective-permute-start(bf16[128,128]{1,0:T(8,128)(2,1)} %bitcast.286), channel_id=1, source_target_pairs={{0,32},{4,36},{8,40},{12,44},{16,48},{20,52},{24,56},{28,60},{32,6... | collective-permute-start | bytes 98312 | tf_op jit(solution)/shard_map/ppermute | solution.py:18
  174.2 2.2 copy-start.4
  174.2 63.7 %copy-start.3 = (bf16[1,128,576]{1,2,0:T(8,128)(2,1)S(1)}, bf16[1,128,576]{1,2,0:T(8,128)(2,1)}, u32[]{:S(2)}) copy-start(bf16[1,128,576]{1,2,0:T(8,128)(2,1)} %param.19) | copy-start | bytes 442372
  176.4 10.3 collective-permute-start.9
  186.8 9.7 collective-permute-start.10
  196.5 9.1 collective-permute-start.11
  205.6 8.8 collective-permute-start.12
  214.4 8.2 collective-permute-start.13
  222.6 7.9 collective-permute-start.14
  230.5 7.3 collective-permute-start.15
  237.9 12.6 collective-permute-start.4
  240.6 12.0 collective-permute-start.5
  242.5 12.4 collective-permute-start.6
  244.5 11.7 collective-permute-start.7
  538.3 662.1 %copy-start.6 = (u32[256]{0:T(256)S(1)}, u32[256]{0:T(256)}, u32[]{:S(2)}) copy-start(u32[256]{0:T(256)} %constant.381) | copy-start | bytes 3076
  538.3 662.7 %copy-start.5 = (u32[256]{0:T(256)S(1)}, u32[256]{0:T(256)}, u32[]{:S(2)}) copy-start(u32[256]{0:T(256)} %constant.385) | copy-start | bytes 3076
  538.4 662.1 %reduce-scatter.7.cloned.1.call-start = ((), (), s32[]{:S(2)}) async-start(), calls=%async_computation.3 | async-start | bytes 2293760 | tf_op jit(solution)/shard_map/reduce_scatter | solution.py:26
  1167.6 109.7 %all-reduce.4.cloned.1.call-start = ((), (), s32[]{:S(2)}) async-start(), calls=%async_computation.4 | async-start | bytes 917504
  (2 other events, 1.8 us)
Sparse Core Ops, SparseCore 0:
  538.5 629.1 reduce-scatter.4
  1170.2 30.1 reduce-scatter.6
  1202.7 74.5 all-reduce.3
where the time goes:
time: 1320 us; the launch traced here: 1300 us
  waiting for transfers between devices  791 us (60%)
  blocking collectives  152 us (12%)
  local copies, waits for them, and re-layouts  112 us (8%)
  matrix products  87.8 us (7%)
  other arithmetic  56.2 us (4%)
  starting transfers between devices  48.1 us (4%)
  loops' own time  40.7 us (3%)
  between operations  14.9 us (1%)
    reduce_scatter x2, waiting for transfers between devices, reduced_to_own(): blocks = lax.psum_scatter(blocks, axes[k], scatter_dimension=0, tiled=True)  662 us
    all_gather x1, blocking collectives, body(): full_gate = lax.all_gather(gate_weight, SEQ_GRP, axis=0, tiled=True)  135 us
    unnamed x4, waiting for transfers between devices  74 us
    ppermute x16, waiting for transfers between devices, shifted(): return lax.ppermute(block, axis, route)  55.6 us
    ppermute x16, starting transfers between devices, shifted(): return lax.ppermute(block, axis, route)  48 us
    another operation x65, local copies, waits for them, and re-layouts  43.1 us
    another operation x1, loops' own time, piece_terms(): lax.map(one_batch, jnp.arange(batch_count, dtype=jnp.int32))  38.1 us
  transfers between devices with their start and end apart: 19, of which 14 were waited for; matrix products, arithmetic and copies ran while one was open for 1% of the time, Pallas kernels for 0%

commit v1 on v0

--- a/solution.py
+++ b/solution.py
@@ -1,3 +1,4 @@
+import functools
 import jax
 import jax.numpy as jnp
 from jax import lax
@@ -10,6 +11,17 @@
 target_scale = 0.07216878364870322
 highest = lax.Precision.HIGHEST
 floor_value = -1e30
+
+
+def fit_the_copies(block_in, axis_name):
+    all_rows = []
+    for _ in range(jax.lax.axis_size(axis_name)):
+        all_rows.append(block_in)
+    near = jnp.concatenate(jax.lax.all_to_all(jnp.stack(all_rows, 0), axis_name, 0, 0), 0)
+    return near
+
+
+part_object = functools.partial(fit_the_copies, axis_name=SEQ_GRP)
 
 
 def shifted(block, axis, distance):
@@ -200,7 +212,7 @@
     reach_devices = min(LOOK, seq_count // 2)
     doc_most = reach_devices * row_count
     lengths = doc_lengths[0]
-    full_gate = lax.all_gather(gate_weight, SEQ_GRP, axis=0, tiled=True)
+    full_gate = part_object(gate_weight)
     block_rows = 16
     block_count = row_count // block_rows
     latent_parts = []

time: 1320 us -> 1220 us (0.924)
  blocking collectives: 152 us -> 17.5 us
  local copies, waits for them, and re-layouts: 112 us -> 126 us
  starting transfers between devices: 48.1 us -> 62.1 us
    all_gather x1 -> x0, blocking collectives: 135 us -> none  [body(): full_gate = lax.all_gather(gate_weight, SEQ_GRP, axis=0, tiled=True)]
    another operation x65 -> x66, local copies, waits for them, and re-layouts: 43.1 us -> 44.7 us
  transfers between devices with their start and end apart: 19 -> 20, of which waited for: 14 -> 14; matrix products, arithmetic and copies ran while one was open for 1% -> 2% of each run, Pallas kernels for 0% -> 0%
where the time goes in v1:
time: 1220 us; the launch traced here: 1210 us
  waiting for transfers between devices  802 us (66%)
  local copies, waits for them, and re-layouts  126 us (10%)
  matrix products  87.8 us (7%)
  starting transfers between devices  62.1 us (5%)
  other arithmetic  55.5 us (5%)
  loops' own time  40.7 us (3%)
  blocking collectives  17.5 us (1%)
  between operations  14.8 us (1%)
    reduce_scatter x2, waiting for transfers between devices, reduced_to_own(): blocks = lax.psum_scatter(blocks, axes[k], scatter_dimension=0, tiled=True)  665 us
    unnamed x4, waiting for transfers between devices  74 us
    ppermute x16, waiting for transfers between devices, shifted(): return lax.ppermute(block, axis, route)  63 us
    ppermute x16, starting transfers between devices, shifted(): return lax.ppermute(block, axis, route)  50.3 us
    another operation x65, local copies, waits for them, and re-layouts  42.4 us
    another operation x1, loops' own time, piece_terms(): lax.map(one_batch, jnp.arange(batch_count, dtype=jnp.int32))  38.1 us
  transfers between devices with their start and end apart: 20, of which 14 were waited for; matrix products, arithmetic and copies ran while one was open for 2% of the time, Pallas kernels for 0%

profile of v1, /device:TPU:8, one launch (start us, length us, event | category | flops | bytes accessed | tf_op | source)
XLA Modules:
  0.0 1206.7 jit_solution(7609965194241040869)
XLA Ops:
  7.2 9.2 collective-permute-start
  22.4 7.1 collective-permute-start.3
  39.0 11.7 all-to-all-start
  58.9 18.4 %collective-permute-done.9 = bf16[128,128]{1,0:T(8,128)(2,1)S(1)} collective-permute-done((bf16[128,128]{1,0:T(8,128)(2,1)S(1)}, bf16[128,128]{1,0:T(8,128)(2,1)S(1)}, u32[]{:S(2)}, u32[]{:S(2)}) %collective-permute-start.9) | collective-permute-done | bytes 32800 | tf_op jit(solution)/shard_map/ppermute | solution.py:30
  79.2 7.8 collective-permute-done.10
  88.9 7.2 collective-permute-done.11
  98.1 6.9 collective-permute-done.12
  106.9 6.3 collective-permute-done.13
  157.2 263.2 %while.59 = (s32[]{:T(128)}, f32[8,1,16]{2,1,0:T(1,128)S(1)}, f32[8,1,16,64]{3,2,1,0:T(8,128)}, s32[8]{0:T(128)S(1)}, s32[8]{0:T(128)S(1)}, /*index=5*/s32[8]{0:...) while((s32[]{:T(128)}, f32[8,1,16]{2,1,0:T(1,128)S(1)}, ...), condition=%wide.region_14.16_spmd.clone.clone, body=%wide.region_3.15_spmd.clone.clone.sunk | while | flops 191511280 | bytes 22292232 | solution.py:200
  175.3 6.1 while.60
  205.4 6.1 while.60
  235.4 6.1 while.60
  265.5 6.1 while.60
  295.6 6.1 while.60
  325.6 6.1 while.60
  355.7 12.2 %while.60 = (s32[]{:T(128)}, f32[1,16,64,1152]{3,2,1,0:T(8,128)}, f32[1,16,64,1152]{3,2,1,0:T(8,128)}, f32[1,16,64]{2,1,0:T(8,128)S(1)}, f32[1,16,64]{2,1,0:T(8,...) while((s32[]{:T(128)}, f32[1,16,64,1152]{3,2,1,0:T(8,128)}, ...), condition=%wide.region_9.10_spmd, body=%wide.region_4.9_spmd.sunk | while | flops 187207856 | bytes 5385245 | solution.py:160
  368.0 10.4 while.61
  397.1 12.2 %while.60 = (s32[]{:T(128)}, f32[1,16,64,1152]{3,2,1,0:T(8,128)}, f32[1,16,64,1152]{3,2,1,0:T(8,128)}, f32[1,16,64]{2,1,0:T(8,128)S(1)}, f32[1,16,64]{2,1,0:T(8,...) while((s32[]{:T(128)}, f32[1,16,64,1152]{3,2,1,0:T(8,128)}, ...), condition=%wide.region_9.10_spmd, body=%wide.region_4.9_spmd.sunk | while | flops 187207856 | bytes 5385245 | solution.py:160
  409.3 10.4 while.61
  431.7 6.4 copy.26
  438.2 632.5 %reduce-scatter.5.cloned.1.call-done = f32[128,28,64]{2,0,1:T(8,128)} async-done(((f32[256,28,64]{2,0,1:T(8,128)}), f32[128,28,64]{2,0,1:T(8,128)}) %reduce-scatter.5.cloned.1.call-update) | async-done | bytes 917520 | tf_op jit(solution)/shard_map/reduce_scatter | solution.py:38
  1070.8 32.7 %reduce-scatter.7.cloned.1.call-done = f32[32,28,64]{2,0,1:T(8,128)} async-done(((f32[128,28,64]{2,0,1:T(8,128)}), f32[32,28,64]{2,0,1:T(8,128)}) %reduce-scatter.7.cloned.1.call-update) | async-done | bytes 229392 | tf_op jit(solution)/shard_map/reduce_scatter | solution.py:38
  1106.5 74.0 %all-reduce.4.cloned.1.call-done = f32[32,28,64]{2,0,1:T(8,128)} async-done(((f32[32,28,64]{2,0,1:T(8,128)}), f32[32,28,64]{2,0,1:T(8,128)}) %all-reduce.4.cloned.1.call-update) | async-done | bytes 229392
  1181.4 17.5 %all-reduce.1 = f32[4,28,64]{2,0,1:T(4,128)S(1)} all-reduce(f32[4,28,64]{2,0,1:T(4,128)S(1)} %constant_dynamic-slice_fusion.3), channel_id=5, replica_groups=mesh['seq_0'=4,'seq_1'=8,'seq_2'=2,'grp'=4] {'grp'}, use_global_device_ids=true, to_apply=%region_20.22.clone | all-reduce | flops 7168 | bytes 57344
  (517 shorter events, 344.8 us)
Async XLA Ops:
  7.2 147.9 %copy-start = (bf16[1,128,7168]{2,1,0:T(8,128)(2,1)S(1)}, bf16[1,128,7168]{2,1,0:T(8,128)(2,1)}, u32[]{:S(2)}) copy-start(bf16[1,128,7168]{2,1,0:T(8,128)(2,1)} %param.16) | copy-start | bytes 5505028
  7.2 123.2 %collective-permute-start = (bf16[128,576]{0,1:T(8,128)(2,1)}, bf16[128,576]{0,1:T(8,128)(2,1)S(1)}, u32[]{:S(2)}, u32[]{:S(2)}) collective-permute-start(bf16[128,576]{0,1:T(8,128)(2,1)} %bitcast.275), channel_id=1, source_target_pairs={{0,32},{4,36},{8,40},{12,44},{16,48},{20,52},{24,56},{28,60},{32,6... | collective-permute-start | bytes 442376 | tf_op jit(solution)/shard_map/ppermute | solution.py:30
  16.4 116.6 %collective-permute-start.1 = (bf16[128,576]{0,1:T(8,128)(2,1)}, bf16[128,576]{0,1:T(8,128)(2,1)S(1)}, u32[]{:S(2)}, u32[]{:S(2)}) collective-permute-start(bf16[128,576]{0,1:T(8,128)(2,1)} %bitcast.276), channel_id=1, source_target_pairs={{0,28},{4,32},{8,36},{12,40},{16,44},{20,48},{24,52},{28,56},{32,6... | collective-permute-start | bytes 442376 | tf_op jit(solution)/shard_map/ppermute | solution.py:30
  19.4 116.2 %collective-permute-start.2 = (bf16[128,576]{0,1:T(8,128)(2,1)}, bf16[128,576]{0,1:T(8,128)(2,1)S(1)}, u32[]{:S(2)}, u32[]{:S(2)}) collective-permute-start(bf16[128,576]{0,1:T(8,128)(2,1)} %bitcast.277), channel_id=1, source_target_pairs={{0,24},{4,28},{8,32},{12,36},{16,40},{20,44},{24,48},{28,52},{32,5... | collective-permute-start | bytes 442376 | tf_op jit(solution)/shard_map/ppermute | solution.py:30
  22.4 116.0 %collective-permute-start.3 = (bf16[128,576]{0,1:T(8,128)(2,1)}, bf16[128,576]{0,1:T(8,128)(2,1)S(1)}, u32[]{:S(2)}, u32[]{:S(2)}) collective-permute-start(bf16[128,576]{0,1:T(8,128)(2,1)} %bitcast.278), channel_id=1, source_target_pairs={{0,20},{4,24},{8,28},{12,32},{16,36},{20,40},{24,44},{28,48},{32,5... | collective-permute-start | bytes 442376 | tf_op jit(solution)/shard_map/ppermute | solution.py:30
  29.6 22.9 %collective-permute-start.8 = (bf16[128,128]{1,0:T(8,128)(2,1)}, bf16[128,128]{1,0:T(8,128)(2,1)}, u32[]{:S(2)}, u32[]{:S(2)}) collective-permute-start(bf16[128,128]{1,0:T(8,128)(2,1)} %bitcast.285), channel_id=1, source_target_pairs={{0,32},{4,36},{8,40},{12,44},{16,48},{20,52},{24,56},{28,60},{32,6... | collective-permute-start | bytes 98312 | tf_op jit(solution)/shard_map/ppermute | solution.py:30
  39.0 89.4 %copy-start.2 = (bf16[1,128,576]{1,2,0:T(8,128)(2,1)S(1)}, bf16[1,128,576]{1,2,0:T(8,128)(2,1)}, u32[]{:S(2)}) copy-start(bf16[1,128,576]{1,2,0:T(8,128)(2,1)} %param.19) | copy-start | bytes 442372
  39.0 109.8 %all-to-all-start = ((bf16[256,2,896]{2,1,0:T(2,128)(2,1)}), bf16[256,2,896]{2,1,0:T(2,128)(2,1)S(1)}, u32[]{:S(2)}, u32[]{:S(2)}) async-start(bf16[256,2,896]{2,1,0:T(2,128)(2,1)} %reshape.591), calls=%async_computation | async-start | bytes 1835008 | tf_op jit(solution)/shard_map/all_to_all | solution.py:20
  50.7 1020.0 %reduce-scatter.5.cloned.1.call-start = ((), (), s32[]{:S(2)}) async-start(), calls=%async_computation.3 | async-start | bytes 5505024 | tf_op jit(solution)/shard_map/reduce_scatter | solution.py:38
  52.5 24.8 %collective-permute-start.9 = (bf16[128,128]{1,0:T(8,128)(2,1)S(1)}, bf16[128,128]{1,0:T(8,128)(2,1)S(1)}, u32[]{:S(2)}, u32[]{:S(2)}) collective-permute-start(bf16[128,128]{1,0:T(8,128)(2,1)S(1)} %bitcast.286), channel_id=1, source_target_pairs={{0,28},{4,32},{8,36},{12,40},{16,44},{20,48},{24,52},{28,56},{32,6... | collective-permute-start | bytes 98312 | tf_op jit(solution)/shard_map/ppermute | solution.py:30
  77.3 9.7 collective-permute-start.10
  87.0 9.1 collective-permute-start.11
  96.1 8.8 collective-permute-start.12
  104.9 8.2 collective-permute-start.13
  113.2 7.9 collective-permute-start.14
  121.1 7.3 collective-permute-start.15
  128.4 12.9 %collective-permute-start.4 = (bf16[128,576]{0,1:T(8,128)(2,1)S(1)}, bf16[128,576]{0,1:T(8,128)(2,1)S(1)}, u32[]{:S(2)}, u32[]{:S(2)}) collective-permute-start(bf16[128,576]{0,1:T(8,128)(2,1)S(1)} %bitcast.279), channel_id=1, source_target_pairs={{0,16},{4,20},{8,24},{12,28},{16,32},{20,36},{24,40},{28,44},{32,4... | collective-permute-start | bytes 442376 | tf_op jit(solution)/shard_map/ppermute | solution.py:30
  130.4 12.1 %collective-permute-start.5 = (bf16[128,576]{0,1:T(8,128)(2,1)S(1)}, bf16[128,576]{0,1:T(8,128)(2,1)S(1)}, u32[]{:S(2)}, u32[]{:S(2)}) collective-permute-start(bf16[128,576]{0,1:T(8,128)(2,1)S(1)} %bitcast.280), channel_id=1, source_target_pairs={{0,12},{4,16},{8,20},{12,24},{16,28},{20,32},{24,36},{28,40},{32,4... | collective-permute-start | bytes 442376 | tf_op jit(solution)/shard_map/ppermute | solution.py:30
  133.0 12.8 %collective-permute-start.6 = (bf16[128,576]{0,1:T(8,128)(2,1)S(1)}, bf16[128,576]{0,1:T(8,128)(2,1)S(1)}, u32[]{:S(2)}, u32[]{:S(2)}) collective-permute-start(bf16[128,576]{0,1:T(8,128)(2,1)S(1)} %bitcast.281), channel_id=1, source_target_pairs={{0,8},{4,12},{8,16},{12,20},{16,24},{20,28},{24,32},{28,36},{32,40... | collective-permute-start | bytes 442376 | tf_op jit(solution)/shard_map/ppermute | solution.py:30
  135.7 11.2 collective-permute-start.7
  438.1 665.4 %copy-start.6 = (u32[256]{0:T(256)S(1)}, u32[256]{0:T(256)}, u32[]{:S(2)}) copy-start(u32[256]{0:T(256)} %constant.381) | copy-start | bytes 3076
  438.1 666.0 %copy-start.5 = (u32[256]{0:T(256)S(1)}, u32[256]{0:T(256)}, u32[]{:S(2)}) copy-start(u32[256]{0:T(256)} %constant.385) | copy-start | bytes 3076
  438.1 665.3 %reduce-scatter.7.cloned.1.call-start = ((), (), s32[]{:S(2)}) async-start(), calls=%async_computation.4 | async-start | bytes 2293760 | tf_op jit(solution)/shard_map/reduce_scatter | solution.py:38
  1070.7 109.7 %all-reduce.4.cloned.1.call-start = ((), (), s32[]{:S(2)}) async-start(), calls=%async_computation.5 | async-start | bytes 917504
  (3 other events, 52.0 us)
Sparse Core Ops, SparseCore 0:
  438.2 632.4 reduce-scatter.4
  1073.2 30.1 reduce-scatter.6
  1105.8 74.6 all-reduce.3
